TPU v7x, 32 devices: a whole 2x2x4 slice. The times are simulated.
32 devices in a mesh: groups: 2 (over y), row: 4 (over z), col: 2 (over x), rep: 2 (over core).
Axes of the slice: x: 2, y: 2, z: 4, core: 2. Of those that a mesh axis runs over, the one named last changes fastest.
Arguments:
- left_panel: float32 [192512, 2048], P(('groups', 'row', 'col', 'rep')), parts along dimension 0, may hold values from -0.02734375 to 0.02734375
- earlier: float32 [192512, 256], P(('groups', 'row', 'col', 'rep')), parts along dimension 0, may hold values from -6 to 6
- diag_block: float32 [4096, 2048], P(('groups', 'col'), 'row'), parts along dimension 0, as said below
- chosen: int32 [512], P(('groups', 'row', 'rep')), parts along dimension 0, may hold values from 0 to 2047
Outputs:
- marginal: float32 [4096, 256], P(('groups', 'col'), ('row', 'rep')), parts along dimension 0
- updated: float32 [192512, 256], P(('groups', 'row', 'col', 'rep')), parts along dimension 0
There are 2 independent parts, one for each index of `groups`. A program takes and returns all parts, laid end to end along the dimension named above; each array names one. Nothing has to cross between parts.
Inputs may be any that keep to these rules, and one draw needn't show every extreme that they name: diag_block is lower triangular with diagonal entries from 1 to 2.
All inputs are finite; a program needn't handle non-finite values.
Results may differ from a plain program's by a relative error of at most 0.00029.
Values sent between devices are 32-bit elements; how exact they have to be, the bound alone decides.
No kernel may reach another device: no remote copies, remote signals or barrier semaphores. Data moves between devices by JAX's collectives and lax.ppermute only.
A program may use at most 192 MiB of HBM per device.

v0:
```python
import jax
import jax.numpy as jnp
from jax import lax
from jax.sharding import PartitionSpec as P

exact_mode = lax.Precision.HIGHEST


def spread(block, axis, holder):
    block = jnp.where(lax.axis_index(axis) == holder, block, jnp.zeros_like(block))
    return lax.psum(block, axis)


def local(left_panel, earlier, diag_block, chosen):
    row_count = lax.axis_size("row")
    col_count = lax.axis_size("col")
    pair_count = lax.axis_size("rep")
    position = lax.axis_index("col")
    local_rows, slab_size = left_panel.shape
    height = slab_size // col_count
    total_cols = earlier.shape[1]
    narrow = total_cols // (row_count * pair_count)
    panel_tiles = left_panel.reshape(local_rows, col_count, height)
    earlier_tiles = earlier.reshape(local_rows, row_count, pair_count, narrow)
    products = jnp.einsum(
        "pca,prqb->rcqab",
        panel_tiles,
        earlier_tiles,
        precision=exact_mode,
        preferred_element_type=jnp.float32,
    )
    products = products.reshape(row_count * col_count * pair_count, height * narrow)
    summed = lax.psum_scatter(products, ("row", "col", "rep"), scatter_dimension=0, tiled=True)
    coupled = summed.reshape(height, narrow)
    rows_here = position * height + jnp.arange(height, dtype=jnp.int32)
    unit_cols = (rows_here[:, None] == chosen[None, :]).astype(jnp.float32)
    right_side = unit_cols - coupled
    row_block = lax.all_gather(diag_block, "row", axis=1, tiled=True)
    diag_tile = lax.dynamic_slice_in_dim(row_block, position * height, height, 1)
    empty = jnp.zeros((height, narrow), jnp.float32)

    def forward_step(level, carry):
        carried, solved = carry
        candidate = lax.linalg.triangular_solve(
            diag_tile, right_side - carried, left_side=True, lower=True
        )
        panel = spread(candidate, "col", level)
        solved = jnp.where(level == position, panel, solved)
        coupling_tile = lax.dynamic_slice_in_dim(row_block, level * height, height, 1)
        update = jnp.dot(
            coupling_tile, panel, precision=exact_mode, preferred_element_type=jnp.float32
        )
        carried = carried + jnp.where(position > level, update, 0.0)
        return (carried, solved)

    carried_fwd, forward = lax.fori_loop(0, col_count, forward_step, (empty, empty))

    def backward_step(counter, carry):
        carried, result = carry
        level = col_count - 1 - counter
        candidate = lax.linalg.triangular_solve(
            diag_tile, forward - carried, left_side=True, lower=True, transpose_a=True
        )
        result = jnp.where(level == position, candidate, result)
        spread_rows = jnp.dot(
            row_block.T, candidate, precision=exact_mode, preferred_element_type=jnp.float32
        )
        spread_rows = spread(spread_rows, "col", level)
        update = lax.dynamic_slice_in_dim(spread_rows, position * height, height, 0)
        carried = carried + jnp.where(position < level, update, 0.0)
        return (carried, result)

    carried_bwd, marginal = lax.fori_loop(0, col_count, backward_step, (empty, empty))
    gathered = lax.all_gather(
        marginal.reshape(1, height * narrow), ("row", "col", "rep"), axis=0, tiled=True
    )
    gathered = gathered.reshape(row_count, col_count, pair_count, height, narrow)
    correction = jnp.einsum(
        "pca,rcqab->prqb",
        panel_tiles,
        gathered,
        precision=exact_mode,
        preferred_element_type=jnp.float32,
    )
    updated = earlier - correction.reshape(local_rows, total_cols)
    return (marginal, updated)


def solution(mesh):
    placed = (
        P(("groups", "row", "col", "rep"), None),
        P(("groups", "row", "col", "rep"), None),
        P(("groups", "col"), "row"),
        P(("groups", "row", "rep")),
    )
    return jax.shard_map(
        local,
        mesh=mesh,
        in_specs=placed,
        out_specs=(P(("groups", "col"), ("row", "rep")), P(("groups", "row", "col", "rep"), None)),
        check_vma=False,
    )
```

profile of v0, /device:TPU:0, one launch (start us, length us, event | category | flops | bytes accessed | tf_op | source)
XLA Modules:
  0.0 1081.9 jit_solution(3599358955177712432)
XLA Ops:
  8.0 6.5 copy.22
  14.6 62.0 %reshape.191 = f32[6016,2,1024]{2,1,0:T(2,128)} reshape(f32[6016,2048]{1,0:T(8,128)} %param.8) | data formatting | bytes 98566144 | tf_op jit(solution)/shard_map/reshape | solution.py:23
  76.6 66.4 %fusion.106 = f32[4,2,2,1024,32]{3,4,1,2,0:T(8,128)S(1)} fusion(f32[6016,4,2,32,1]{0,3,4,2,1:T(8,128)} %bitcast.282, f32[6016,2,1024,1,1]{2,1,0,4,3:T(2,128)} %bitcast.280), kind=kOutput, calls=%fused_computation.192 | convolution fusion | flops 37849399296 | bytes 57540608 | tf_op jit(solution)/shard_map/pca,prqb->rcqab/dot_general | solution.py:25
  143.0 4.6 copy.24
  147.6 7.0 reshape.192
  155.8 232.2 %all-reduce.5.cloned.1.call-done = f32[16,32768]{1,0:T(8,128)} async-done(((f32[16,32768]{1,0:T(8,128)}), f32[16,32768]{1,0:T(8,128)}) %all-reduce.5.cloned.1.call-update) | async-done | bytes 2097168
  388.1 2.2 dynamic-slice_reduce_fusion
  390.9 6.9 fusion.105
  397.8 23.6 %while.41 = (s32[]{:T(128)}, f32[1024,1024]{1,0:T(8,128)}, s32[8,2]{0,1:T(2,128)S(1)}, f32[8,128,128]{2,1,0:T(8,128)S(1)}, s32[]{:T(128)}) while((s32[]{:T(128)}, f32[1024,1024]{1,0:T(8,128)}, s32[8,2]{0,1:T(2,128)S(1)}, f32[8,128,128]{2,1,0:T(8,128)S(1)}, s32[]{:T(128)}) %tuple.158), condition=%wide.while_cond, body=%wide.while_body.sunk | while | flops 2 | bytes 131189 | solution.py:44
  398.5 2.3 bitcast_dynamic-update-slice_fusion.2
  401.4 2.3 bitcast_dynamic-update-slice_fusion.2
  404.4 2.3 bitcast_dynamic-update-slice_fusion.2
  407.3 2.3 bitcast_dynamic-update-slice_fusion.2
  410.3 2.3 bitcast_dynamic-update-slice_fusion.2
  413.3 2.3 bitcast_dynamic-update-slice_fusion.2
  416.2 2.3 bitcast_dynamic-update-slice_fusion.2
  419.2 2.2 bitcast_dynamic-update-slice_fusion.2
  421.4 78.6 %custom-call.21 = f32[8,128,128]{1,2,0:T(8,128)S(1)} custom-call(f32[8,128,128]{2,1,0:T(8,128)S(1)} %get-tuple-element.500), custom_call_target="InvertDiagBlocksLowerTriangular" | custom-call | tf_op jit(solution)/shard_map/while/body/eval_jaxpr/triangular_solve | solution.py:44
  500.2 89.2 %while.42 = (s32[]{:T(128)}, f32[1024,32]{0,1:T(8,128)S(1)}, f32[1024,32]{0,1:T(8,128)S(1)}, s32[]{:T(128)}, f32[1024,2048]{1,0:T(8,128)}, /*index=5*/f32[1024,3...) while((s32[]{:T(128)}, f32[1024,32]{0,1:T(8,128)S(1)}, ...), condition=%wide.region_3.4_spmd.clone, body=%wide.region_1.3_spmd.clone.sunk | while | flops 631648256 | bytes 18481448 | solution.py:56
  500.3 4.8 fusion.223
  511.0 1.4 convolution_subtract_fusion.32
  512.7 1.5 convolution_subtract_fusion.33
  514.4 1.6 convolution_subtract_fusion.34
  516.9 20.9 %all-reduce.7.cloned.1.call-done = f32[1024,32]{0,1:T(8,128)} async-done(((f32[1024,32]{0,1:T(8,128)}), f32[1024,32]{0,1:T(8,128)}) %all-reduce.7.cloned.1.call-update) | async-done | bytes 131088 | tf_op jit(solution)/shard_map/while/body/eval_jaxpr/psum | solution.py:11
  538.8 6.1 fusion.225
  544.9 4.8 fusion.223
  555.7 1.4 convolution_subtract_fusion.32
  557.3 1.5 convolution_subtract_fusion.33
  559.0 1.6 convolution_subtract_fusion.34
  561.6 21.7 %all-reduce.7.cloned.1.call-done = f32[1024,32]{0,1:T(8,128)} async-done(((f32[1024,32]{0,1:T(8,128)}), f32[1024,32]{0,1:T(8,128)}) %all-reduce.7.cloned.1.call-update) | async-done | bytes 131088 | tf_op jit(solution)/shard_map/while/body/eval_jaxpr/psum | solution.py:11
  583.3 6.1 fusion.225
  589.4 96.0 %while.43 = (s32[]{:T(128)}, f32[1024,32]{0,1:T(8,128)S(1)}, f32[1024,32]{0,1:T(8,128)S(1)}, s32[]{:T(128)}, f32[1024,32]{0,1:T(8,128)S(1)}, /*index=5*/f32[1024...) while((s32[]{:T(128)}, f32[1024,32]{0,1:T(8,128)S(1)}, ...), condition=%wide.region_6.7_spmd.clone, body=%wide.region_4.6_spmd.clone.sunk | while | flops 1034366976 | bytes 24002808 | solution.py:73
  589.9 4.8 fusion.255
  601.6 1.3 convolution_subtract_fusion.40
  603.2 1.4 convolution_subtract_fusion.41
  604.9 7.9 fusion.258
  612.8 24.3 %all-reduce.9.cloned.1.call-done = f32[2048,32]{0,1:T(8,128)} async-done(((f32[2048,32]{0,1:T(8,128)}), f32[2048,32]{0,1:T(8,128)}) %all-reduce.9.cloned.1.call-update) | async-done | bytes 262160 | tf_op jit(solution)/shard_map/while/body/eval_jaxpr/psum | solution.py:11
  638.1 4.8 fusion.255
  649.9 1.3 convolution_subtract_fusion.40
  651.4 1.4 convolution_subtract_fusion.41
  653.1 7.9 fusion.258
  661.1 23.4 %all-reduce.9.cloned.1.call-done = f32[2048,32]{0,1:T(8,128)} async-done(((f32[2048,32]{0,1:T(8,128)}), f32[2048,32]{0,1:T(8,128)}) %all-reduce.9.cloned.1.call-update) | async-done | bytes 262160 | tf_op jit(solution)/shard_map/while/body/eval_jaxpr/psum | solution.py:11
  686.6 43.5 %all-gather.6.cloned.1.call-done = f32[16,1,32768]{2,1,0:T(1,128)} async-done(((f32[1,1,32768]{2,1,0:T(1,128)}), f32[16,1,32768]{2,1,0:T(1,128)}) %all-gather.6.cloned.1.call-update) | async-done | bytes 2097168 | tf_op jit(solution)/shard_map/all_gather | solution.py:74
  730.2 6.6 reduce.1
  736.8 4.7 reshape.195
  741.5 318.1 %fusion.100 = f32[4,2,32,6016,1]{3,2,1,4,0:T(8,128)} fusion(f32[4,2,2,1024,32]{4,3,2,1,0:T(8,128)} %reshape.195, f32[6016,2,1024,1,1]{2,1,0,4,3:T(2,128)} %bitcast.281), kind=kOutput, calls=%fused_computation.185 | convolution fusion | flops 37849399296 | bytes 57540608 | tf_op jit(solution)/shard_map/pca,rcqab->prqb/dot_general | solution.py:78
  1059.7 6.5 copy.31
  1066.2 8.0 sub.41
  (158 shorter events, 40.3 us)
Async XLA Ops:
  8.0 380.1 %all-reduce.5.cloned.1.call-start = ((), (), s32[]{:S(2)}) async-start(), calls=%async_computation.2 | async-start | bytes 4194304
  154.5 0.7 copy-start.2
  154.5 235.9 %copy-start.1 = (s32[32]{0:T(128)S(1)}, s32[32]{0:T(128)}, u32[]{:S(2)}) copy-start(s32[32]{0:T(128)} %param.11) | copy-start | bytes 388
  154.6 236.3 %all-gather.4.cloned.1.call-start = ((), (), s32[]{:S(2)}) async-start(), calls=%async_computation | async-start | bytes 10485760 | tf_op jit(solution)/shard_map/all_gather | solution.py:38
  500.2 37.6 %all-reduce.7.cloned.1.call-start = ((), (), s32[]{:S(2)}) async-start(), calls=%async_computation.3 | async-start | bytes 262144 | tf_op jit(solution)/shard_map/while/body/eval_jaxpr/psum | solution.py:11
  544.9 38.3 %all-reduce.7.cloned.1.call-start = ((), (), s32[]{:S(2)}) async-start(), calls=%async_computation.3 | async-start | bytes 262144 | tf_op jit(solution)/shard_map/while/body/eval_jaxpr/psum | solution.py:11
  589.8 47.3 %all-reduce.9.cloned.1.call-start = ((), (), s32[]{:S(2)}) async-start(), calls=%async_computation.4 | async-start | bytes 524288 | tf_op jit(solution)/shard_map/while/body/eval_jaxpr/psum | solution.py:11
  638.1 46.4 %all-reduce.9.cloned.1.call-start = ((), (), s32[]{:S(2)}) async-start(), calls=%async_computation.4 | async-start | bytes 524288 | tf_op jit(solution)/shard_map/while/body/eval_jaxpr/psum | solution.py:11
  685.4 56.1 %copy-start = (f32[1024,32]{0,1:T(8,128)}, f32[1024,32]{0,1:T(8,128)S(1)}, u32[]{:S(2)}) copy-start(f32[1024,32]{0,1:T(8,128)S(1)} %get-tuple-element.489) | copy-start | bytes 393220
  685.4 44.7 %all-gather.6.cloned.1.call-start = ((), (), s32[]{:S(2)}) async-start(), calls=%async_computation.1 | async-start | bytes 2228224 | tf_op jit(solution)/shard_map/all_gather | solution.py:74
Sparse Core Ops, SparseCore 0:
  154.7 233.3 all-reduce.4
  517.0 20.7 all-reduce.6
  561.7 21.5 all-reduce.6
  612.9 24.1 all-reduce.8
  661.1 23.2 all-reduce.8
  688.7 41.4 all-gather.5
Sparse Core Ops, SparseCore 1:
  156.6 157.0 all-gather.3
where the time goes:
time: 1090 us; the launch traced here: 1080 us
  matrix products  454 us (42%)
  waiting for transfers between devices  367 us (34%)
  other arithmetic  124 us (11%)
  local copies, waits for them, and re-layouts  120 us (11%)
  between operations  15.9 us (1%)
    dot_general x1, matrix products, local(): jnp.einsum('pca,rcqab->prqb', panel_tiles, gathered, precision=exact_mode...  318 us
    unnamed x4, waiting for transfers between devices  233 us
    another operation x5, other arithmetic, forward_step(): lax.linalg.triangular_solve(diag_tile, right_side - carried, left_side=Tr...  95.1 us
    psum x4, waiting for transfers between devices, spread(): return lax.psum(block, axis)  90.3 us
    dot_general x1, matrix products, local(): jnp.einsum('pca,prqb->rcqab', panel_tiles, earlier_tiles, precision=exact...  66.4 us
    reshape x1, local copies, waits for them, and re-layouts, local(): panel_tiles = left_panel.reshape(local_rows, col_count, height)  62 us
    all_gather x1, waiting for transfers between devices, local(): lax.all_gather(marginal.reshape(1, height * narrow), ('row', 'col', 'rep'...  43.5 us
    another operation x24, local copies, waits for them, and re-layouts  23.4 us
  transfers between devices with their start and end apart: 7, of which 6 were waited for; matrix products, arithmetic and copies ran while one was open for 0% of the time, Pallas kernels for 0%

commit v1 on v0

--- a/solution.py
+++ b/solution.py
@@ -8,7 +8,7 @@
 
 def spread(block, axis, holder):
     block = jnp.where(lax.axis_index(axis) == holder, block, jnp.zeros_like(block))
-    return lax.psum(block, axis)
+    return jnp.sum(lax.all_gather(block, axis), axis=0)
 
 
 def local(left_panel, earlier, diag_block, chosen):

time: 1090 us -> 1000 us (0.917)
  waiting for transfers between devices: 367 us -> 273 us
  blocking collectives: 0 us -> 25.4 us
  matrix products: 454 us -> 439 us
    psum x4 -> x0, waiting for transfers between devices: 90.3 us -> none  [spread(): return lax.psum(block, axis)]
    all_gather x0 -> x4, blocking collectives: none -> 25.4 us  [spread(): return jnp.sum(lax.all_gather(block, axis), axis=0)]
    another operation x30, matrix products: 22 us -> 8.47 us  [forward_step(): lax.linalg.triangular_solve(diag_tile, right_side - carried, left_side=Tr...]
  transfers between devices with their start and end apart: 7 -> 3, of which waited for: 6 -> 2; matrix products, arithmetic and copies ran while one was open for 0% -> 0% of each run, Pallas kernels for 0% -> 0%
where the time goes in v1:
time: 1000 us; the launch traced here: 992 us
  matrix products  439 us (44%)
  waiting for transfers between devices  273 us (27%)
  local copies, waits for them, and re-layouts  119 us (12%)
  other arithmetic  117 us (12%)
  blocking collectives  25.4 us (3%)
  between operations  15.8 us (2%)
    dot_general x1, matrix products, local(): jnp.einsum('pca,rcqab->prqb', panel_tiles, gathered, precision=exact_mode...  318 us
    unnamed x4, waiting for transfers between devices  233 us
    another operation x5, other arithmetic, forward_step(): lax.linalg.triangular_solve(diag_tile, right_side - carried, left_side=Tr...  90.8 us
    dot_general x1, matrix products, local(): jnp.einsum('pca,prqb->rcqab', panel_tiles, earlier_tiles, precision=exact...  66.4 us
    reshape x1, local copies, waits for them, and re-layouts, local(): panel_tiles = left_panel.reshape(local_rows, col_count, height)  62 us
    all_gather x1, waiting for transfers between devices, local(): lax.all_gather(marginal.reshape(1, height * narrow), ('row', 'col', 'rep'...  40.9 us
    all_gather x4, blocking collectives, spread(): return jnp.sum(lax.all_gather(block, axis), axis=0)  25.4 us
    another operation x24, local copies, waits for them, and re-layouts  22.2 us
  transfers between devices with their start and end apart: 3, of which 2 were waited for; matrix products, arithmetic and copies ran while one was open for 0% of the time, Pallas kernels for 0%

profile of v1, /device:TPU:0, one launch (start us, length us, event | category | flops | bytes accessed | tf_op | source)
XLA Modules:
  0.0 992.1 jit_solution(8300861370746132185)
XLA Ops:
  8.0 6.5 copy.22
  14.6 62.0 %reshape.338 = f32[6016,2,1024]{2,1,0:T(2,128)} reshape(f32[6016,2048]{1,0:T(8,128)} %param.8) | data formatting | bytes 98566144 | tf_op jit(solution)/shard_map/reshape | solution.py:23
  76.6 66.4 %fusion.112 = f32[4,2,2,1024,32]{3,4,1,2,0:T(8,128)S(1)} fusion(f32[6016,4,2,32,1]{0,3,4,2,1:T(8,128)} %bitcast.347, f32[6016,2,1024,1,1]{2,1,0,4,3:T(2,128)} %bitcast.345), kind=kOutput, calls=%fused_computation.192 | convolution fusion | flops 37849399296 | bytes 57540608 | tf_op jit(solution)/shard_map/pca,prqb->rcqab/dot_general | solution.py:25
  143.0 4.6 copy.24
  147.6 7.0 reshape.339
  156.1 232.0 %all-reduce.3.cloned.1.call-done = f32[16,32768]{1,0:T(8,128)} async-done(((f32[16,32768]{1,0:T(8,128)}), f32[16,32768]{1,0:T(8,128)}) %all-reduce.3.cloned.1.call-update) | async-done | bytes 2097168
  388.1 2.1 dynamic-slice_reduce_fusion
  390.8 6.9 fusion.111
  397.8 22.4 %while.41 = (s32[]{:T(128)}, f32[1024,1024]{1,0:T(8,128)}, s32[8,2]{0,1:T(2,128)S(1)}, f32[8,128,128]{2,1,0:T(8,128)S(1)}, s32[]{:T(128)}) while((s32[]{:T(128)}, f32[1024,1024]{1,0:T(8,128)}, s32[8,2]{0,1:T(2,128)S(1)}, f32[8,128,128]{2,1,0:T(8,128)S(1)}, s32[]{:T(128)}) %tuple.166), condition=%wide.while_cond, body=%wide.while_body.sunk | while | flops 2 | bytes 131189 | solution.py:44
  398.4 2.2 bitcast_dynamic-update-slice_fusion.2
  401.2 2.2 bitcast_dynamic-update-slice_fusion.2
  404.0 2.2 bitcast_dynamic-update-slice_fusion.2
  406.8 2.2 bitcast_dynamic-update-slice_fusion.2
  409.6 2.2 bitcast_dynamic-update-slice_fusion.2
  412.4 2.2 bitcast_dynamic-update-slice_fusion.2
  415.2 2.2 bitcast_dynamic-update-slice_fusion.2
  418.0 2.1 bitcast_dynamic-update-slice_fusion.2
  420.1 78.6 %custom-call.21 = f32[8,128,128]{1,2,0:T(8,128)S(1)} custom-call(f32[8,128,128]{2,1,0:T(8,128)S(1)} %get-tuple-element.500), custom_call_target="InvertDiagBlocksLowerTriangular" | custom-call | tf_op jit(solution)/shard_map/while/body/eval_jaxpr/triangular_solve | solution.py:44
  498.9 38.2 %while.42 = (s32[]{:T(128)}, f32[1024,32]{0,1:T(8,128)S(1)}, f32[1024,32]{0,1:T(8,128)S(1)}, s32[]{:T(128)}, f32[1024,2048]{1,0:T(8,128)}, /*index=5*/f32[1024,3...) while((s32[]{:T(128)}, f32[1024,32]{0,1:T(8,128)S(1)}, ...), condition=%wide.region_3.4_spmd.clone, body=%wide.region_1.3_spmd.clone.sunk | while | flops 631648256 | bytes 18645260 | solution.py:56
  499.2 2.7 fusion.229
  506.2 5.6 all_gather.47
  511.9 6.1 fusion.231
  518.3 2.7 fusion.229
  525.3 5.6 all_gather.47
  531.0 6.1 fusion.231
  537.1 61.2 %while.43 = (s32[]{:T(128)}, f32[1024,32]{0,1:T(8,128)S(1)}, f32[1024,32]{0,1:T(8,128)S(1)}, s32[]{:T(128)}, f32[1024,32]{0,1:T(8,128)S(1)}, /*index=5*/f32[1024...) while((s32[]{:T(128)}, f32[1024,32]{0,1:T(8,128)S(1)}, ...), condition=%wide.region_6.7_spmd.clone, body=%wide.region_4.6_spmd.clone.sunk | while | flops 1034366976 | bytes 25051364 | solution.py:73
  537.5 4.8 fusion.261
  544.9 1.2 convolution_subtract_fusion.37
  546.3 1.2 convolution_subtract_fusion.38
  547.8 1.3 convolution_subtract_fusion.39
  549.3 1.3 convolution_subtract_fusion.40
  550.9 1.4 convolution_subtract_fusion.41
  552.5 7.2 fusion.264
  559.7 7.0 all-gather.4
  567.9 4.8 fusion.261
  575.4 1.2 convolution_subtract_fusion.37
  576.7 1.2 convolution_subtract_fusion.38
  578.2 1.3 convolution_subtract_fusion.39
  579.7 1.3 convolution_subtract_fusion.40
  581.3 1.4 convolution_subtract_fusion.41
  582.9 7.2 fusion.264
  590.1 7.0 all-gather.4
  599.5 40.9 %all-gather.10.cloned.1.call-done = f32[16,1,32768]{2,1,0:T(1,128)} async-done(((f32[1,1,32768]{2,1,0:T(1,128)}), f32[16,1,32768]{2,1,0:T(1,128)}) %all-gather.10.cloned.1.call-update) | async-done | bytes 2097168 | tf_op jit(solution)/shard_map/all_gather | solution.py:74
  640.4 6.6 reduce.1
  647.0 4.7 reshape.342
  651.8 318.1 %fusion.106 = f32[4,2,32,6016,1]{3,2,1,4,0:T(8,128)} fusion(f32[4,2,2,1024,32]{4,3,2,1,0:T(8,128)} %reshape.342, f32[6016,2,1024,1,1]{2,1,0,4,3:T(2,128)} %bitcast.346), kind=kOutput, calls=%fused_computation.185 | convolution fusion | flops 37849399296 | bytes 57540608 | tf_op jit(solution)/shard_map/pca,rcqab->prqb/dot_general | solution.py:78
  969.9 6.5 copy.31
  976.5 8.0 sub.41
  (170 shorter events, 26.3 us)
Async XLA Ops:
  8.0 380.1 %all-reduce.3.cloned.1.call-start = ((), (), s32[]{:S(2)}) async-start(), calls=%async_computation.2 | async-start | bytes 4194304
  154.5 0.9 copy-start.2
  154.5 235.9 %copy-start.1 = (s32[32]{0:T(128)S(1)}, s32[32]{0:T(128)}, u32[]{:S(2)}) copy-start(s32[32]{0:T(128)} %param.11) | copy-start | bytes 388
  154.6 236.2 %all-gather.8.cloned.1.call-start = ((), (), s32[]{:S(2)}) async-start(), calls=%async_computation | async-start | bytes 10485760 | tf_op jit(solution)/shard_map/all_gather | solution.py:38
  155.2 485.2 %all-gather.10.cloned.1.call-start = ((), (), s32[]{:S(2)}) async-start(), calls=%async_computation.1 | async-start | bytes 2228224 | tf_op jit(solution)/shard_map/all_gather | solution.py:74
  598.4 53.4 %copy-start = (f32[1024,32]{0,1:T(8,128)}, f32[1024,32]{0,1:T(8,128)S(1)}, u32[]{:S(2)}) copy-start(f32[1024,32]{0,1:T(8,128)S(1)} %get-tuple-element.489) | copy-start | bytes 393220
Sparse Core Ops, SparseCore 0:
  154.7 233.3 all-reduce.2
  599.6 40.7 all-gather.9
Sparse Core Ops, SparseCore 1:
  156.6 157.0 all-gather.7
